TPU v7x, 32 devices: a whole 2x2x4 slice. The times are simulated.
32 devices in a mesh: seq: 8 (over z, y), rows: 4 (over x, core).
Axes of the slice: x: 2, y: 2, z: 4, core: 2. Of those that a mesh axis runs over, the one named last changes fastest.
Arguments:
- hidden: bfloat16 [4, 1024, 768], P('rows', 'seq'), may hold values from -6 to 6
- cotangent: bfloat16 [4, 1024, 768], P('rows', 'seq'), may hold values from -6 to 6
- segment_ids: int32 [4, 1024], P('rows', 'seq'), may hold values from 0 to 15, never falling along the last dimension, each value on 1 to 768 neighbouring positions
- timesteps: int32 [4, 16], P('rows'), may hold values from 0 to 4999
- qkv_weight: bfloat16 [768, 2304], replicated, may hold values from -0.21875 to 0.21875
- qv_bias: float32 [1536], replicated, may hold values from -3 to 3
- out_weight: bfloat16 [768, 768], replicated, may hold values from -1.75 to 1.75
- out_bias: float32 [768], replicated, may hold values from -3 to 3
- up_weight: bfloat16 [768, 3072], replicated, may hold values from -0.21875 to 0.21875
- up_bias: float32 [3072], replicated, may hold values from -3 to 3
- down_weight: bfloat16 [3072, 768], replicated, may hold values from -0.109375 to 0.109375
- down_bias: float32 [768], replicated, may hold values from -3 to 3
- norm_gain: float32 [2, 768], replicated, may hold values from 0.1 to 1.9
- norm_bias: float32 [2, 768], replicated, may hold values from -3 to 3
- time_weight: bfloat16 [768, 768], replicated, may hold values from -0.21875 to 0.21875
Outputs:
- result: bfloat16 [4, 1024, 768], P('rows', 'seq')
- input_grad: float32 [4, 1024, 768], P('rows', 'seq')
- grad_qkv_weight: float32 [768, 2304], P('seq')
- grad_qv_bias: float32 [1536], P('seq')
- grad_out_weight: float32 [768, 768], P('seq')
- grad_out_bias: float32 [768], P('seq')
- grad_up_weight: float32 [768, 3072], P('seq')
- grad_up_bias: float32 [3072], P('seq')
- grad_down_weight: float32 [3072, 768], P('seq')
- grad_down_bias: float32 [768], P('seq')
- grad_norm_gain: float32 [2, 768], P(None, 'seq')
- grad_norm_bias: float32 [2, 768], P(None, 'seq')
- grad_time_weight: float32 [768, 768], P('seq')
Inputs may be any that keep to these rules, and one draw needn't show every extreme that they name: `segment_ids`: along each row the ids never fall; each of the 16 documents covers 1 to 768 consecutive tokens, and one of each row covers exactly 768.
All inputs are finite; a program needn't handle non-finite values.
Results may differ from a plain program's by a relative error of at most 0.023.
Values may be sent and summed in bfloat16 or wider, within the bound.
No kernel may reach another device: no remote copies, remote signals or barrier semaphores. Data moves between devices by JAX's collectives and lax.ppermute only.
A program may use at most 192 MiB of HBM per device.

v0:
```python
import math
import jax
import jax.numpy as jnp
from jax import lax
from jax.sharding import PartitionSpec as P

D = 768
H = 12
HD = 64
DOCS = 16
EPS = 1e-05
NEG_BIG = -1e30
precise = lax.Precision.HIGHEST


def shifted(block, axis, distance):
    devices = range(lax.axis_size(axis))
    route = [((i - distance) % len(devices), i) for i in devices]
    return lax.ppermute(block, axis, route)


def time_features(timesteps):
    half_width = D // 2
    frequency = jnp.exp(
        jnp.arange(half_width, dtype=jnp.float32) * (-math.log(10000.0) / half_width)
    )
    phases = timesteps.astype(jnp.float32)[..., None] * frequency
    return jnp.concatenate([jnp.sin(phases), jnp.cos(phases)], axis=-1)


def layer_norm(residual, gain_row, offset):
    average = jnp.mean(residual, axis=-1, keepdims=True)
    centered = residual - average
    inverse = lax.rsqrt(jnp.mean(centered * centered, axis=-1, keepdims=True) + EPS)
    return centered * inverse * gain_row + offset


def gelu_exact(values):
    return jax.nn.gelu(values, approximate=False)


def divisor_under(total, limit):
    chosen = 1
    for candidate in range(1, min(total, limit) + 1):
        if total % candidate == 0:
            chosen = candidate
    return chosen


def body(
    hidden,
    cotangent,
    segment_ids,
    timesteps,
    qkv_weight,
    qv_bias,
    out_weight,
    out_bias,
    up_weight,
    up_bias,
    down_weight,
    down_bias,
    norm_gain,
    norm_bias,
    time_weight,
):
    row_count = hidden.shape[0]
    seq_rows = hidden.shape[1]
    tokens = row_count * seq_rows
    score_scale = HD ** (-0.5)
    all_docs = lax.all_gather(segment_ids, "seq", axis=1, tiled=True)
    features = time_features(timesteps).astype(jnp.bfloat16)
    doc_embed = jnp.einsum("rkd,de->rke", features, time_weight, preferred_element_type=jnp.float32)
    onehot = (segment_ids[..., None] == jnp.arange(DOCS, dtype=jnp.int32)).astype(jnp.float32)
    embedded = jnp.einsum("rsk,rke->rse", onehot, doc_embed, precision=precise)
    inputs = (hidden.astype(jnp.float32) + embedded).reshape(tokens, D)
    inputs_low = inputs.astype(jnp.bfloat16)
    projected = jnp.dot(inputs_low, qkv_weight, preferred_element_type=jnp.float32)
    queries = (projected[:, :D] + qv_bias[:D]).astype(jnp.bfloat16)
    keys_own = projected[:, D : 2 * D].astype(jnp.bfloat16).reshape(row_count, seq_rows, D)
    values_own = (
        (projected[:, 2 * D :] + qv_bias[D:]).astype(jnp.bfloat16).reshape(row_count, seq_rows, D)
    )
    query_heads = queries.reshape(row_count, seq_rows, H, HD)
    initial = (
        jnp.full((row_count, H, seq_rows), NEG_BIG, jnp.float32),
        jnp.zeros((row_count, H, seq_rows), jnp.float32),
        jnp.zeros((row_count, H, seq_rows, HD), jnp.float32),
    )
    fold_state = initial
    key_piece = lax.all_gather(keys_own, "seq", axis=1, tiled=True)
    value_piece = lax.all_gather(values_own, "seq", axis=1, tiled=True)
    width_keys = key_piece.shape[1]
    block_rows = divisor_under(width_keys, 1024)
    block_count = width_keys // block_rows
    key_blocks = jnp.moveaxis(key_piece.reshape(row_count, block_count, block_rows, H, HD), 1, 0)
    value_blocks = jnp.moveaxis(
        value_piece.reshape(row_count, block_count, block_rows, H, HD), 1, 0
    )
    doc_blocks = jnp.moveaxis(all_docs.reshape(row_count, block_count, block_rows), 1, 0)

    def absorb(run_state, block_item):
        run_max, run_sum, run_acc = run_state
        key_block, value_block, doc_block = block_item
        scores = (
            jnp.einsum(
                "rqhd,rkhd->rhqk", query_heads, key_block, preferred_element_type=jnp.float32
            )
            * score_scale
        )
        same_doc = segment_ids[:, None, :, None] == doc_block[:, None, None, :]
        new_max = jnp.maximum(run_max, jnp.max(jnp.where(same_doc, scores, NEG_BIG), axis=-1))
        weights = jnp.where(same_doc, jnp.exp(scores - new_max[..., None]), 0.0)
        factor = jnp.exp(run_max - new_max)
        run_sum = run_sum * factor + jnp.sum(weights, axis=-1)
        run_acc = run_acc * factor[..., None] + jnp.einsum(
            "rhqk,rkhd->rhqd",
            weights.astype(jnp.bfloat16),
            value_block,
            preferred_element_type=jnp.float32,
        )
        return ((new_max, run_sum, run_acc), None)

    fold_state, _ = lax.scan(absorb, fold_state, (key_blocks, value_blocks, doc_blocks))
    run_max, run_sum, run_acc = fold_state
    attended_heads = run_acc / run_sum[..., None]
    log_total = run_max + jnp.log(run_sum)
    attended = jnp.transpose(attended_heads, (0, 2, 1, 3)).reshape(tokens, D)
    attended_low = attended.astype(jnp.bfloat16)
    branch = jnp.dot(attended_low, out_weight, preferred_element_type=jnp.float32) + out_bias
    normed_one, first_pull = jax.vjp(layer_norm, inputs + branch, norm_gain[0], norm_bias[0])
    first_low = normed_one.astype(jnp.bfloat16)
    up_values = jnp.dot(first_low, up_weight, preferred_element_type=jnp.float32) + up_bias
    activated, gelu_pull = jax.vjp(gelu_exact, up_values)
    activated_low = activated.astype(jnp.bfloat16)
    ffn_out = jnp.dot(activated_low, down_weight, preferred_element_type=jnp.float32) + down_bias
    output, second_pull = jax.vjp(layer_norm, normed_one + ffn_out, norm_gain[1], norm_bias[1])
    result = output.astype(jnp.bfloat16).reshape(row_count, seq_rows, D)
    grad_second, gain_two, bias_two = second_pull(cotangent.astype(jnp.float32).reshape(tokens, D))
    down_low = grad_second.astype(jnp.bfloat16)
    grad_down_weight = jnp.einsum(
        "nf,nd->fd", activated_low, down_low, preferred_element_type=jnp.float32
    )
    grad_down_bias = jnp.sum(down_low.astype(jnp.float32), axis=0)
    activ_grad = jnp.einsum("nd,fd->nf", down_low, down_weight, preferred_element_type=jnp.float32)
    upper_low = gelu_pull(activ_grad)[0].astype(jnp.bfloat16)
    grad_up_weight = jnp.einsum(
        "nd,nf->df", first_low, upper_low, preferred_element_type=jnp.float32
    )
    grad_up_bias = jnp.sum(upper_low.astype(jnp.float32), axis=0)
    grad_first = grad_second + jnp.einsum(
        "nf,df->nd", upper_low, up_weight, preferred_element_type=jnp.float32
    )
    grad_resid, gain_one, bias_one = first_pull(grad_first)
    branch_low = grad_resid.astype(jnp.bfloat16)
    grad_out_weight = jnp.einsum(
        "nd,ne->de", attended_low, branch_low, preferred_element_type=jnp.float32
    )
    grad_out_bias = jnp.sum(branch_low.astype(jnp.float32), axis=0)
    attn_grad_low = jnp.einsum(
        "ne,de->nd", branch_low, out_weight, preferred_element_type=jnp.float32
    ).astype(jnp.bfloat16)
    grad_heads = attn_grad_low.reshape(row_count, seq_rows, H, HD)
    row_delta = jnp.einsum(
        "rqhd,rhqd->rhq", grad_heads.astype(jnp.float32), attended_heads, precision=precise
    )

    def block_grads(key_heads, value_heads, block_docs):
        width_keys = key_heads.shape[1]
        scores = (
            jnp.einsum(
                "rqhd,rkhd->rhqk", query_heads, key_heads, preferred_element_type=jnp.float32
            )
            * score_scale
        )
        same_doc = segment_ids[:, None, :, None] == block_docs[:, None, None, :]
        probabilities = jnp.where(same_doc, jnp.exp(scores - log_total[..., None]), 0.0)
        probs_low = probabilities.astype(jnp.bfloat16)
        value_part = jnp.einsum(
            "rhqk,rqhd->rkhd", probs_low, grad_heads, preferred_element_type=jnp.float32
        ).reshape(row_count, width_keys, D)
        prob_grad = jnp.einsum(
            "rqhd,rkhd->rhqk", grad_heads, value_heads, preferred_element_type=jnp.float32
        )
        score_low = (probabilities * (prob_grad - row_delta[..., None])).astype(jnp.bfloat16)
        query_part = (
            jnp.einsum("rhqk,rkhd->rqhd", score_low, key_heads, preferred_element_type=jnp.float32)
            * score_scale
        )
        key_part = (
            jnp.einsum(
                "rhqk,rqhd->rkhd", score_low, query_heads, preferred_element_type=jnp.float32
            )
            * score_scale
        ).reshape(row_count, width_keys, D)
        return (query_part, key_part, value_part)

    my_index = lax.axis_index("seq")
    cycle_size = lax.axis_size("seq")

    def cycle_turn(turn_index, cycle_state):
        key_block, value_block, key_grad, value_grad, query_grad = cycle_state
        anchor = (my_index - turn_index + cycle_size) % cycle_size
        block_docs = lax.dynamic_slice_in_dim(all_docs, anchor * seq_rows, seq_rows, 1)
        query_part, key_part, value_part = block_grads(
            key_block.reshape(row_count, seq_rows, H, HD),
            value_block.reshape(row_count, seq_rows, H, HD),
            block_docs,
        )
        query_grad = query_grad + query_part
        key_grad = key_grad + key_part
        value_grad = value_grad + value_part
        key_block, value_block = shifted((key_block, value_block), "seq", 1)
        key_grad, value_grad = (
            shifted(key_grad.astype(jnp.bfloat16), "seq", 1).astype(key_grad.dtype),
            shifted(value_grad.astype(jnp.bfloat16), "seq", 1).astype(value_grad.dtype),
        )
        return (key_block, value_block, key_grad, value_grad, query_grad)

    cycle_init = (
        keys_own,
        values_own,
        jnp.zeros((row_count, seq_rows, D), jnp.float32),
        jnp.zeros((row_count, seq_rows, D), jnp.float32),
        jnp.zeros((row_count, seq_rows, H, HD), jnp.float32),
    )
    cycle_done = lax.fori_loop(0, cycle_size, cycle_turn, cycle_init)
    query_total, key_total, value_total = (cycle_done[4], cycle_done[2], cycle_done[3])
    query_low = query_total.reshape(tokens, D).astype(jnp.bfloat16)
    key_low = key_total.reshape(tokens, D).astype(jnp.bfloat16)
    value_low = value_total.reshape(tokens, D).astype(jnp.bfloat16)
    packed = jnp.concatenate([query_low, key_low, value_low], axis=1)
    grad_qkv_weight = jnp.einsum(
        "nd,ne->de", inputs_low, packed, preferred_element_type=jnp.float32
    )
    grad_qv_bias = jnp.concatenate(
        [
            jnp.sum(query_low.astype(jnp.float32), axis=0),
            jnp.sum(value_low.astype(jnp.float32), axis=0),
        ]
    )
    input_grad = grad_resid + jnp.einsum(
        "ne,de->nd", packed, qkv_weight, preferred_element_type=jnp.float32
    )
    input_grad = input_grad.reshape(row_count, seq_rows, D)
    doc_grad = jnp.einsum("rsk,rsd->rkd", onehot, input_grad, precision=precise)
    grad_time_weight = jnp.einsum(
        "rkd,rke->de", features.astype(jnp.float32), doc_grad, precision=precise
    )
    grad_norm_gain = jnp.stack([gain_one, gain_two])
    grad_norm_bias = jnp.stack([bias_one, bias_two])
    local_grads = (
        grad_qkv_weight,
        grad_qv_bias,
        grad_out_weight,
        grad_out_bias,
        grad_up_weight,
        grad_up_bias,
        grad_down_weight,
        grad_down_bias,
        grad_norm_gain,
        grad_norm_bias,
        grad_time_weight,
    )
    stacked_flags = (False, False, False, False, False, False, False, False, True, True, False)
    seq_count = lax.axis_size("seq")
    laid_out = []
    for grad_piece, stacked in zip(local_grads, stacked_flags):
        if stacked:
            laid_out.append(
                jnp.transpose(grad_piece.reshape(2, seq_count, -1), (1, 0, 2)).reshape(
                    seq_count, -1
                )
            )
        else:
            laid_out.append(grad_piece.reshape(seq_count, -1))
    flat_grads = jnp.concatenate(laid_out, axis=1)
    share_width = flat_grads.shape[1]
    row_count_axis = lax.axis_size("rows")
    padding = -share_width % row_count_axis
    split_rows = flat_grads.reshape(
        seq_count * row_count_axis, (share_width + padding) // row_count_axis
    )
    shares = lax.psum_scatter(split_rows, ("seq", "rows"), scatter_dimension=0, tiled=True)
    whole = lax.all_gather(shares.astype(jnp.bfloat16), "rows", axis=0, tiled=True).astype(
        shares.dtype
    )
    mine = whole.reshape(-1)
    outputs_list = [result, input_grad]
    position = 0
    for grad_piece, stacked in zip(local_grads, stacked_flags):
        count = grad_piece.size // seq_count
        segment = mine[position : position + count]
        if stacked:
            outputs_list.append(segment.reshape(2, grad_piece.shape[1] // seq_count))
        else:
            outputs_list.append(
                segment.reshape((grad_piece.shape[0] // seq_count,) + grad_piece.shape[1:])
            )
        position += count
    return tuple(outputs_list)


def solution(mesh):
    return jax.shard_map(
        body,
        mesh=mesh,
        in_specs=(
            P("rows", "seq", None),
            P("rows", "seq", None),
            P("rows", "seq"),
            P("rows", None),
            P(),
            P(),
            P(),
            P(),
            P(),
            P(),
            P(),
            P(),
            P(),
            P(),
            P(),
        ),
        out_specs=(
            P("rows", "seq", None),
            P("rows", "seq", None),
            P("seq", None),
            P("seq"),
            P("seq", None),
            P("seq"),
            P("seq", None),
            P("seq"),
            P("seq", None),
            P("seq"),
            P(None, "seq"),
            P(None, "seq"),
            P("seq", None),
        ),
        check_vma=False,
    )
```

profile of v0, /device:TPU:0, one launch (start us, length us, event | category | flops | bytes accessed | tf_op | source)
XLA Modules:
  0.0 1149.3 jit_solution(14988583280119527673)
XLA Ops:
  24.3 22.2 %all_gather.14 = s32[1,1024]{1,0:T(1,128)S(1)} all-gather(s32[1,128]{1,0:T(1,128)S(1)} %copy-done.36), channel_id=1, replica_groups=mesh['seq'=8,'rows'=4] {'seq'}, dimensions={1}, use_global_device_ids=true | all-gather | bytes 4608 | tf_op jit(solution)/shard_map/all_gather | solution.py:71
  48.8 11.9 %all-gather.7.cloned.1.call-done = bf16[1024,768]{1,0:T(8,128)(2,1)} async-done(((bf16[128,768]{1,0:T(8,128)(2,1)}), bf16[1024,768]{1,0:T(8,128)(2,1)}) %all-gather.7.cloned.1.call-update) | async-done | bytes 1572880 | tf_op jit(solution)/shard_map/all_gather | solution.py:91
  69.9 36.6 %all-gather.9.cloned.1.call-done = bf16[1024,768]{1,0:T(8,128)(2,1)} async-done(((bf16[128,768]{1,0:T(8,128)(2,1)}), bf16[1024,768]{1,0:T(8,128)(2,1)}) %all-gather.9.cloned.1.call-update) | async-done | bytes 1572880 | tf_op jit(solution)/shard_map/all_gather | solution.py:92
  109.3 5.7 fusion.83
  134.9 193.8 %while.30 = (s32[]{:T(128)}, bf16[1,128,768]{1,2,0:T(8,128)(2,1)}, bf16[1,128,768]{1,2,0:T(8,128)(2,1)}, f32[1,128,768]{1,2,0:T(8,128)}, f32[1,128,768]{1,2,0:T(...) while((s32[]{:T(128)}, bf16[1,128,768]{1,2,0:T(8,128)(2,1)}, ...), condition=%wide.region_11.12_spmd.clone, body=%wide.region_10.11_spmd.clone.sunk | while | flops 128401424 | bytes 19905180 | solution.py:227
  152.6 5.1 collective-permute-done.2
  293.8 5.6 collective-permute-done.2
  317.9 6.1 collective-permute-done.2
  340.8 5.0 fusion.72
  345.8 5.0 fusion.87
  350.8 7.1 reshape.640
  357.9 5.5 constant_dynamic-update-slice_fusion.1
  365.8 8.9 reshape.643
  374.8 8.9 reshape.645
  392.0 7.5 dynamic-update-slice.2
  401.0 26.5 %dynamic-update-slice.4 = f32[8,959616]{1,0:T(8,128)} dynamic-update-slice(f32[8,959616]{1,0:T(8,128)} %dynamic-update-slice.3, f32[8,294912]{1,0:T(8,128)} %reshape.643, s32[]{} %constant.210, s32[]{} %constant.215) | dynamic-update-slice | bytes 18874372
  428.9 26.6 %dynamic-update-slice.6 = f32[8,959616]{1,0:T(8,128)} dynamic-update-slice(f32[8,959616]{1,0:T(8,128)} %dynamic-update-slice.5, f32[8,294912]{1,0:T(8,128)} %reshape.645, s32[]{} %constant.210, s32[]{} %constant.217) | dynamic-update-slice | bytes 18874372
  461.5 37.1 %reshape.681 = f32[7676928]{0:T(1024)} reshape(f32[8,959616]{1,0:T(8,128)} %constant_dynamic-update-slice_fusion) | data formatting | bytes 61415424
  498.6 41.0 %reshape.650 = f32[32,239904]{1,0:T(8,128)} reshape(f32[7676928]{0:T(1024)} %reshape.681) | data formatting | bytes 61415424 | tf_op jit(solution)/shard_map/reshape | solution.py:281
  539.6 492.5 %all-reduce.2 = bf16[32,239904]{1,0:T(8,128)(2,1)} all-reduce(f32[32,239904]{1,0:T(8,128)} %reshape.650), channel_id=4, replica_groups=mesh['seq'=8,'rows'=4] {'seq','rows'}, use_global_device_ids=true, to_apply=%region_21.22.clone | all-reduce | flops 7676928 | bytes 46061568
  1035.5 29.7 %all-gather.11.cloned.1.call-done = bf16[4,1,239904]{2,1,0:T(2,128)(2,1)} async-done(((bf16[1,1,239904]{2,1,0:T(2,128)(2,1)}), bf16[4,1,239904]{2,1,0:T(2,128)(2,1)}) %all-gather.11.cloned.1.call-update) | async-done | bytes 1919248 | tf_op jit(solution)/shard_map/all_gather | solution.py:285
  1065.2 43.7 %convert_reduce_fusion = f32[4,239904]{1,0:T(4,128)} fusion(bf16[4,1,239904]{2,1,0:T(2,128)(2,1)} %all-gather.11.cloned.1.call-done), kind=kLoop, calls=%fused_computation.27 | loop fusion | flops 959616 | bytes 5757696 | tf_op jit(solution)/shard_map/convert_element_type | solution.py:285
  1108.8 6.5 reshape.651
  1124.2 8.4 slice.82
  (463 shorter events, 280.3 us)
Async XLA Ops:
  7.2 53.5 %all-gather.7.cloned.1.call-start = ((), (), s32[]{:S(2)}) async-start(), calls=%async_computation | async-start | bytes 1769472 | tf_op jit(solution)/shard_map/all_gather | solution.py:91
  13.6 92.8 %all-gather.9.cloned.1.call-start = ((), (), s32[]{:S(2)}) async-start(), calls=%async_computation.1 | async-start | bytes 1769472 | tf_op jit(solution)/shard_map/all_gather | solution.py:92
  15.7 1049.5 %all-gather.11.cloned.1.call-start = ((), (), s32[]{:S(2)}) async-start(), calls=%async_computation.2 | async-start | bytes 4800000 | tf_op jit(solution)/shard_map/all_gather | solution.py:285
  136.7 24.8 %collective-permute-start = (bf16[1,128,768]{1,2,0:T(8,128)(2,1)}, bf16[1,128,768]{1,2,0:T(8,128)(2,1)}, u32[]{:S(2)}, u32[]{:S(2)}) collective-permute-start(bf16[1,128,768]{1,2,0:T(8,128)(2,1)} %copy.66), channel_id=1, source_target_pairs={{28,0},{0,4},{4,8},{8,12},{12,16},{16,20},{20,24},{24,28},{29,1},{... | collective-permute-start | bytes 589832 | tf_op jit(solution)/shard_map/while/body/eval_jaxpr/ppermute | solution.py:19
  138.9 22.6 %collective-permute-start.1 = (bf16[1,128,768]{1,2,0:T(8,128)(2,1)}, bf16[1,128,768]{1,2,0:T(8,128)(2,1)}, u32[]{:S(2)}, u32[]{:S(2)}) collective-permute-start(bf16[1,128,768]{1,2,0:T(8,128)(2,1)} %copy.67), channel_id=1, source_target_pairs={{28,0},{0,4},{4,8},{8,12},{12,16},{16,20},{20,24},{24,28},{29,1},{... | collective-permute-start | bytes 589832 | tf_op jit(solution)/shard_map/while/body/eval_jaxpr/ppermute | solution.py:19
  163.1 21.9 %collective-permute-start = (bf16[1,128,768]{1,2,0:T(8,128)(2,1)}, bf16[1,128,768]{1,2,0:T(8,128)(2,1)}, u32[]{:S(2)}, u32[]{:S(2)}) collective-permute-start(bf16[1,128,768]{1,2,0:T(8,128)(2,1)} %copy.66), channel_id=1, source_target_pairs={{28,0},{0,4},{4,8},{8,12},{12,16},{16,20},{20,24},{24,28},{29,1},{... | collective-permute-start | bytes 589832 | tf_op jit(solution)/shard_map/while/body/eval_jaxpr/ppermute | solution.py:19
  164.8 20.2 %collective-permute-start.1 = (bf16[1,128,768]{1,2,0:T(8,128)(2,1)}, bf16[1,128,768]{1,2,0:T(8,128)(2,1)}, u32[]{:S(2)}, u32[]{:S(2)}) collective-permute-start(bf16[1,128,768]{1,2,0:T(8,128)(2,1)} %copy.67), channel_id=1, source_target_pairs={{28,0},{0,4},{4,8},{8,12},{12,16},{16,20},{20,24},{24,28},{29,1},{... | collective-permute-start | bytes 589832 | tf_op jit(solution)/shard_map/while/body/eval_jaxpr/ppermute | solution.py:19
  171.9 11.3 collective-permute-start.3
  186.6 21.5 %collective-permute-start = (bf16[1,128,768]{1,2,0:T(8,128)(2,1)}, bf16[1,128,768]{1,2,0:T(8,128)(2,1)}, u32[]{:S(2)}, u32[]{:S(2)}) collective-permute-start(bf16[1,128,768]{1,2,0:T(8,128)(2,1)} %copy.66), channel_id=1, source_target_pairs={{28,0},{0,4},{4,8},{8,12},{12,16},{16,20},{20,24},{24,28},{29,1},{... | collective-permute-start | bytes 589832 | tf_op jit(solution)/shard_map/while/body/eval_jaxpr/ppermute | solution.py:19
  188.2 19.9 %collective-permute-start.1 = (bf16[1,128,768]{1,2,0:T(8,128)(2,1)}, bf16[1,128,768]{1,2,0:T(8,128)(2,1)}, u32[]{:S(2)}, u32[]{:S(2)}) collective-permute-start(bf16[1,128,768]{1,2,0:T(8,128)(2,1)} %copy.67), channel_id=1, source_target_pairs={{28,0},{0,4},{4,8},{8,12},{12,16},{16,20},{20,24},{24,28},{29,1},{... | collective-permute-start | bytes 589832 | tf_op jit(solution)/shard_map/while/body/eval_jaxpr/ppermute | solution.py:19
  194.9 11.6 %collective-permute-start.3 = (bf16[1,128,768]{1,2,0:T(8,128)(2,1)}, bf16[1,128,768]{1,2,0:T(8,128)(2,1)}, u32[]{:S(2)}, u32[]{:S(2)}) collective-permute-start(bf16[1,128,768]{1,2,0:T(8,128)(2,1)} %fusion.148), channel_id=1, source_target_pairs={{28,0},{0,4},{4,8},{8,12},{12,16},{16,20},{20,24},{24,28},{29,1},{... | collective-permute-start | bytes 589832 | tf_op jit(solution)/shard_map/while/body/eval_jaxpr/ppermute | solution.py:19
  209.8 21.8 %collective-permute-start = (bf16[1,128,768]{1,2,0:T(8,128)(2,1)}, bf16[1,128,768]{1,2,0:T(8,128)(2,1)}, u32[]{:S(2)}, u32[]{:S(2)}) collective-permute-start(bf16[1,128,768]{1,2,0:T(8,128)(2,1)} %copy.66), channel_id=1, source_target_pairs={{28,0},{0,4},{4,8},{8,12},{12,16},{16,20},{20,24},{24,28},{29,1},{... | collective-permute-start | bytes 589832 | tf_op jit(solution)/shard_map/while/body/eval_jaxpr/ppermute | solution.py:19
  211.4 20.1 %collective-permute-start.1 = (bf16[1,128,768]{1,2,0:T(8,128)(2,1)}, bf16[1,128,768]{1,2,0:T(8,128)(2,1)}, u32[]{:S(2)}, u32[]{:S(2)}) collective-permute-start(bf16[1,128,768]{1,2,0:T(8,128)(2,1)} %copy.67), channel_id=1, source_target_pairs={{28,0},{0,4},{4,8},{8,12},{12,16},{16,20},{20,24},{24,28},{29,1},{... | collective-permute-start | bytes 589832 | tf_op jit(solution)/shard_map/while/body/eval_jaxpr/ppermute | solution.py:19
  233.1 22.1 %collective-permute-start = (bf16[1,128,768]{1,2,0:T(8,128)(2,1)}, bf16[1,128,768]{1,2,0:T(8,128)(2,1)}, u32[]{:S(2)}, u32[]{:S(2)}) collective-permute-start(bf16[1,128,768]{1,2,0:T(8,128)(2,1)} %copy.66), channel_id=1, source_target_pairs={{28,0},{0,4},{4,8},{8,12},{12,16},{16,20},{20,24},{24,28},{29,1},{... | collective-permute-start | bytes 589832 | tf_op jit(solution)/shard_map/while/body/eval_jaxpr/ppermute | solution.py:19
  234.8 20.5 %collective-permute-start.1 = (bf16[1,128,768]{1,2,0:T(8,128)(2,1)}, bf16[1,128,768]{1,2,0:T(8,128)(2,1)}, u32[]{:S(2)}, u32[]{:S(2)}) collective-permute-start(bf16[1,128,768]{1,2,0:T(8,128)(2,1)} %copy.67), channel_id=1, source_target_pairs={{28,0},{0,4},{4,8},{8,12},{12,16},{16,20},{20,24},{24,28},{29,1},{... | collective-permute-start | bytes 589832 | tf_op jit(solution)/shard_map/while/body/eval_jaxpr/ppermute | solution.py:19
  256.9 22.5 %collective-permute-start = (bf16[1,128,768]{1,2,0:T(8,128)(2,1)}, bf16[1,128,768]{1,2,0:T(8,128)(2,1)}, u32[]{:S(2)}, u32[]{:S(2)}) collective-permute-start(bf16[1,128,768]{1,2,0:T(8,128)(2,1)} %copy.66), channel_id=1, source_target_pairs={{28,0},{0,4},{4,8},{8,12},{12,16},{16,20},{20,24},{24,28},{29,1},{... | collective-permute-start | bytes 589832 | tf_op jit(solution)/shard_map/while/body/eval_jaxpr/ppermute | solution.py:19
  258.5 20.9 %collective-permute-start.1 = (bf16[1,128,768]{1,2,0:T(8,128)(2,1)}, bf16[1,128,768]{1,2,0:T(8,128)(2,1)}, u32[]{:S(2)}, u32[]{:S(2)}) collective-permute-start(bf16[1,128,768]{1,2,0:T(8,128)(2,1)} %copy.67), channel_id=1, source_target_pairs={{28,0},{0,4},{4,8},{8,12},{12,16},{16,20},{20,24},{24,28},{29,1},{... | collective-permute-start | bytes 589832 | tf_op jit(solution)/shard_map/while/body/eval_jaxpr/ppermute | solution.py:19
  265.6 12.1 %collective-permute-start.3 = (bf16[1,128,768]{1,2,0:T(8,128)(2,1)}, bf16[1,128,768]{1,2,0:T(8,128)(2,1)}, u32[]{:S(2)}, u32[]{:S(2)}) collective-permute-start(bf16[1,128,768]{1,2,0:T(8,128)(2,1)} %fusion.148), channel_id=1, source_target_pairs={{28,0},{0,4},{4,8},{8,12},{12,16},{16,20},{20,24},{24,28},{29,1},{... | collective-permute-start | bytes 589832 | tf_op jit(solution)/shard_map/while/body/eval_jaxpr/ppermute | solution.py:19
  281.1 23.0 %collective-permute-start = (bf16[1,128,768]{1,2,0:T(8,128)(2,1)}, bf16[1,128,768]{1,2,0:T(8,128)(2,1)}, u32[]{:S(2)}, u32[]{:S(2)}) collective-permute-start(bf16[1,128,768]{1,2,0:T(8,128)(2,1)} %copy.66), channel_id=1, source_target_pairs={{28,0},{0,4},{4,8},{8,12},{12,16},{16,20},{20,24},{24,28},{29,1},{... | collective-permute-start | bytes 589832 | tf_op jit(solution)/shard_map/while/body/eval_jaxpr/ppermute | solution.py:19
  282.7 21.4 %collective-permute-start.1 = (bf16[1,128,768]{1,2,0:T(8,128)(2,1)}, bf16[1,128,768]{1,2,0:T(8,128)(2,1)}, u32[]{:S(2)}, u32[]{:S(2)}) collective-permute-start(bf16[1,128,768]{1,2,0:T(8,128)(2,1)} %copy.67), channel_id=1, source_target_pairs={{28,0},{0,4},{4,8},{8,12},{12,16},{16,20},{20,24},{24,28},{29,1},{... | collective-permute-start | bytes 589832 | tf_op jit(solution)/shard_map/while/body/eval_jaxpr/ppermute | solution.py:19
  289.4 13.0 %collective-permute-start.3 = (bf16[1,128,768]{1,2,0:T(8,128)(2,1)}, bf16[1,128,768]{1,2,0:T(8,128)(2,1)}, u32[]{:S(2)}, u32[]{:S(2)}) collective-permute-start(bf16[1,128,768]{1,2,0:T(8,128)(2,1)} %fusion.148), channel_id=1, source_target_pairs={{28,0},{0,4},{4,8},{8,12},{12,16},{16,20},{20,24},{24,28},{29,1},{... | collective-permute-start | bytes 589832 | tf_op jit(solution)/shard_map/while/body/eval_jaxpr/ppermute | solution.py:19
  305.7 23.0 %collective-permute-start = (bf16[1,128,768]{1,2,0:T(8,128)(2,1)}, bf16[1,128,768]{1,2,0:T(8,128)(2,1)}, u32[]{:S(2)}, u32[]{:S(2)}) collective-permute-start(bf16[1,128,768]{1,2,0:T(8,128)(2,1)} %copy.66), channel_id=1, source_target_pairs={{28,0},{0,4},{4,8},{8,12},{12,16},{16,20},{20,24},{24,28},{29,1},{... | collective-permute-start | bytes 589832 | tf_op jit(solution)/shard_map/while/body/eval_jaxpr/ppermute | solution.py:19
  307.3 21.4 %collective-permute-start.1 = (bf16[1,128,768]{1,2,0:T(8,128)(2,1)}, bf16[1,128,768]{1,2,0:T(8,128)(2,1)}, u32[]{:S(2)}, u32[]{:S(2)}) collective-permute-start(bf16[1,128,768]{1,2,0:T(8,128)(2,1)} %copy.67), channel_id=1, source_target_pairs={{28,0},{0,4},{4,8},{8,12},{12,16},{16,20},{20,24},{24,28},{29,1},{... | collective-permute-start | bytes 589832 | tf_op jit(solution)/shard_map/while/body/eval_jaxpr/ppermute | solution.py:19
  313.7 13.2 %collective-permute-start.3 = (bf16[1,128,768]{1,2,0:T(8,128)(2,1)}, bf16[1,128,768]{1,2,0:T(8,128)(2,1)}, u32[]{:S(2)}, u32[]{:S(2)}) collective-permute-start(bf16[1,128,768]{1,2,0:T(8,128)(2,1)} %fusion.148), channel_id=1, source_target_pairs={{28,0},{0,4},{4,8},{8,12},{12,16},{16,20},{20,24},{24,28},{29,1},{... | collective-permute-start | bytes 589832 | tf_op jit(solution)/shard_map/while/body/eval_jaxpr/ppermute | solution.py:19
  (110 other events, 536.3 us)
Sparse Core Ops, SparseCore 0:
  13.8 46.8 all-gather.6
  63.4 42.9 all-gather.8
  1035.6 29.5 all-gather.10
where the time goes:
time: 1160 us; the launch traced here: 1150 us
  blocking collectives  515 us (44%)
  local copies, waits for them, and re-layouts  275 us (24%)
  waiting for transfers between devices  124 us (11%)
  other arithmetic  105 us (9%)
  matrix products  90.3 us (8%)
  starting transfers between devices  25.1 us (2%)
  between operations  14.7 us (1%)
    unnamed x1, blocking collectives  492 us
    unnamed x130, local copies, waits for them, and re-layouts  122 us
    ppermute x32, waiting for transfers between devices, shifted(): return lax.ppermute(block, axis, route)  45.3 us
    convert_element_type x1, other arithmetic, body(): lax.all_gather(shares.astype(jnp.bfloat16), 'rows', axis=0, tiled=True)  43.7 us
    reshape x1, local copies, waits for them, and re-layouts, body(): flat_grads.reshape(seq_count * row_count_axis, (share_width + padding) //...  41 us
    all_gather x1, waiting for transfers between devices, body(): value_piece = lax.all_gather(values_own, 'seq', axis=1, tiled=True)  36.6 us
    reshape x8, local copies, waits for them, and re-layouts, body(): laid_out.append(grad_piece.reshape(seq_count, -1))  30.7 us
    all_gather x1, waiting for transfers between devices, body(): lax.all_gather(shares.astype(jnp.bfloat16), 'rows', axis=0, tiled=True)  29.7 us
  transfers between devices with their start and end apart: 35, of which 19 were waited for; matrix products, arithmetic and copies ran while one was open for 11% of the time, Pallas kernels for 0%

commit v1 on v0

--- a/solution.py
+++ b/solution.py
@@ -11,6 +11,24 @@
 EPS = 1e-05
 NEG_BIG = -1e30
 precise = lax.Precision.HIGHEST
+
+
+def in_order(blocks, dim):
+    shape = list(blocks.shape[1:])
+    shape[dim] *= blocks.shape[0]
+    return jnp.moveaxis(blocks, 0, dim).reshape(shape)
+
+
+def grow_blocks(value, axis):
+    size = lax.axis_size(axis)
+    blocks = value[None]
+    for level in range(size.bit_length() - 1):
+        apart = 1 << level
+        partner_block = lax.ppermute(blocks, axis, [(i, i ^ apart) for i in range(size)])
+        both = jnp.stack([blocks, partner_block])
+        upper = lax.axis_index(axis) >> level & 1
+        blocks = jnp.where(upper == 0, both, both[::-1]).reshape(-1, *value.shape)
+    return blocks
 
 
 def shifted(block, axis, distance):
@@ -89,7 +107,7 @@
     )
     fold_state = initial
     key_piece = lax.all_gather(keys_own, "seq", axis=1, tiled=True)
-    value_piece = lax.all_gather(values_own, "seq", axis=1, tiled=True)
+    value_piece = in_order(grow_blocks(values_own, "seq"), 1)
     width_keys = key_piece.shape[1]
     block_rows = divisor_under(width_keys, 1024)
     block_count = width_keys // block_rows

time: 1160 us -> 1160 us (level)
  waiting for transfers between devices: 124 us -> 83 us
  starting transfers between devices: 25.1 us -> 51.6 us
    all_gather x1 -> x0, waiting for transfers between devices: 36.6 us -> none  [body(): value_piece = lax.all_gather(values_own, 'seq', axis=1, tiled=True)]
    ppermute x0 -> x3, waiting for transfers between devices: none -> 27 us  [grow_blocks(): lax.ppermute(blocks, axis, [(i, i ^ apart) for i in range(size)])]
    ppermute x32, waiting for transfers between devices: 45.3 us -> 25.3 us  [shifted(): return lax.ppermute(block, axis, route)]
    ppermute x32, starting transfers between devices: 25 us -> 44.3 us  [shifted(): return lax.ppermute(block, axis, route)]
    all_gather x1, waiting for transfers between devices: 11.9 us -> 0.01 us  [body(): key_piece = lax.all_gather(keys_own, 'seq', axis=1, tiled=True)]
    unnamed x130 -> x128, local copies, waits for them, and re-layouts: 122 us -> 122 us
  transfers between devices with their start and end apart: 35 -> 37, of which waited for: 19 -> 20; matrix products, arithmetic and copies ran while one was open for 11% -> 12% of each run, Pallas kernels for 0% -> 0%
where the time goes in v1:
time: 1160 us; the launch traced here: 1150 us
  blocking collectives  519 us (45%)
  local copies, waits for them, and re-layouts  279 us (24%)
  other arithmetic  112 us (10%)
  matrix products  86.9 us (7%)
  waiting for transfers between devices  83 us (7%)
  starting transfers between devices  51.6 us (4%)
  between operations  14.9 us (1%)
    unnamed x1, blocking collectives  491 us
    unnamed x128, local copies, waits for them, and re-layouts  122 us
    ppermute x32, starting transfers between devices, shifted(): return lax.ppermute(block, axis, route)  44.3 us
    convert_element_type x1, other arithmetic, body(): lax.all_gather(shares.astype(jnp.bfloat16), 'rows', axis=0, tiled=True)  43.7 us
    reshape x1, local copies, waits for them, and re-layouts, body(): flat_grads.reshape(seq_count * row_count_axis, (share_width + padding) //...  41 us
    reshape x8, local copies, waits for them, and re-layouts, body(): laid_out.append(grad_piece.reshape(seq_count, -1))  30.7 us
    all_gather x1, waiting for transfers between devices, body(): lax.all_gather(shares.astype(jnp.bfloat16), 'rows', axis=0, tiled=True)  30.6 us
    all_gather x1, blocking collectives, body(): all_docs = lax.all_gather(segment_ids, 'seq', axis=1, tiled=True)  28.4 us
  transfers between devices with their start and end apart: 37, of which 20 were waited for; matrix products, arithmetic and copies ran while one was open for 12% of the time, Pallas kernels for 0%

profile of v1, /device:TPU:0, one launch (start us, length us, event | category | flops | bytes accessed | tf_op | source)
XLA Modules:
  0.0 1147.2 jit_solution(12963509451318854085)
XLA Ops:
  18.6 5.2 collective-permute-done.4
  27.6 14.5 %collective-permute-done.5 = bf16[2,1,128,768]{3,2,0,1:T(8,128)(2,1)} collective-permute-done((bf16[2,1,128,768]{3,2,0,1:T(8,128)(2,1)}, bf16[2,1,128,768]{3,2,0,1:T(8,128)(2,1)}, u32[]{:S(2)}, u32[]{:S(2)}) %collective-permute-start.5) | collective-permute-done | bytes 393248 | tf_op jit(solution)/shard_map/ppermute | solution.py:27
  55.3 28.4 %all_gather.11 = s32[1,1024]{1,0:T(1,128)S(1)} all-gather(s32[1,128]{1,0:T(1,128)S(1)} %copy-done.36), channel_id=1, replica_groups=mesh['seq'=8,'rows'=4] {'seq'}, dimensions={1}, use_global_device_ids=true | all-gather | bytes 4608 | tf_op jit(solution)/shard_map/all_gather | solution.py:89
  85.8 7.4 collective-permute-done.6
  115.0 4.2 multiply_convert_fusion
  134.1 193.1 %while.30 = (s32[]{:T(128)}, bf16[1,128,768]{1,2,0:T(8,128)(2,1)}, bf16[1,128,768]{1,2,0:T(8,128)(2,1)}, f32[1,128,768]{1,2,0:T(8,128)}, f32[1,128,768]{1,2,0:T(...) while((s32[]{:T(128)}, bf16[1,128,768]{1,2,0:T(8,128)(2,1)}, ...), condition=%wide.region_11.12_spmd.clone, body=%wide.region_10.11_spmd.clone.sunk | while | flops 128401424 | bytes 19905180 | solution.py:245
  136.0 9.9 collective-permute-start
  333.4 4.0 fusion.49
  339.3 5.0 fusion.74
  344.4 5.0 fusion.89
  349.4 7.1 reshape.648
  356.5 5.5 constant_dynamic-update-slice_fusion.1
  364.3 8.9 reshape.651
  373.3 8.9 reshape.653
  390.6 7.5 dynamic-update-slice.2
  399.5 26.5 %dynamic-update-slice.4 = f32[8,959616]{1,0:T(8,128)} dynamic-update-slice(f32[8,959616]{1,0:T(8,128)} %dynamic-update-slice.3, f32[8,294912]{1,0:T(8,128)} %reshape.651, s32[]{} %constant.214, s32[]{} %constant.219) | dynamic-update-slice | bytes 18874372
  427.5 26.6 %dynamic-update-slice.6 = f32[8,959616]{1,0:T(8,128)} dynamic-update-slice(f32[8,959616]{1,0:T(8,128)} %dynamic-update-slice.5, f32[8,294912]{1,0:T(8,128)} %reshape.653, s32[]{} %constant.214, s32[]{} %constant.221) | dynamic-update-slice | bytes 18874372
  460.0 37.1 %reshape.687 = f32[7676928]{0:T(1024)} reshape(f32[8,959616]{1,0:T(8,128)} %constant_dynamic-update-slice_fusion) | data formatting | bytes 61415424
  497.2 41.0 %reshape.658 = f32[32,239904]{1,0:T(8,128)} reshape(f32[7676928]{0:T(1024)} %reshape.687) | data formatting | bytes 61415424 | tf_op jit(solution)/shard_map/reshape | solution.py:299
  538.1 490.6 %all-reduce.2 = bf16[32,239904]{1,0:T(8,128)(2,1)} all-reduce(f32[32,239904]{1,0:T(8,128)} %reshape.658), channel_id=3, replica_groups=mesh['seq'=8,'rows'=4] {'seq','rows'}, use_global_device_ids=true, to_apply=%region_21.22.clone | all-reduce | flops 7676928 | bytes 46061568
  1032.1 30.6 %all-gather.7.cloned.1.call-done = bf16[4,1,239904]{2,1,0:T(2,128)(2,1)} async-done(((bf16[1,1,239904]{2,1,0:T(2,128)(2,1)}), bf16[4,1,239904]{2,1,0:T(2,128)(2,1)}) %all-gather.7.cloned.1.call-update) | async-done | bytes 1919248 | tf_op jit(solution)/shard_map/all_gather | solution.py:303
  1062.7 43.7 %convert_reduce_fusion = f32[4,239904]{1,0:T(4,128)} fusion(bf16[4,1,239904]{2,1,0:T(2,128)(2,1)} %all-gather.7.cloned.1.call-done), kind=kLoop, calls=%fused_computation.27 | loop fusion | flops 959616 | bytes 5757696 | tf_op jit(solution)/shard_map/convert_element_type | solution.py:303
  1106.4 6.5 reshape.659
  1121.8 8.4 slice.82
  (471 shorter events, 298.8 us)
Async XLA Ops:
  7.2 96.6 %all-gather.5.cloned.1.call-start = ((), (), s32[]{:S(2)}) async-start(), calls=%async_computation | async-start | bytes 1769472 | tf_op jit(solution)/shard_map/all_gather | solution.py:109
  13.6 1049.1 %all-gather.7.cloned.1.call-start = ((), (), s32[]{:S(2)}) async-start(), calls=%async_computation.1 | async-start | bytes 4800000 | tf_op jit(solution)/shard_map/all_gather | solution.py:303
  25.8 16.3 %collective-permute-start.5 = (bf16[2,1,128,768]{3,2,0,1:T(8,128)(2,1)}, bf16[2,1,128,768]{3,2,0,1:T(8,128)(2,1)}, u32[]{:S(2)}, u32[]{:S(2)}) collective-permute-start(bf16[2,1,128,768]{3,2,0,1:T(8,128)(2,1)} %get-tuple-element.498), channel_id=1, source_target_pairs={{0,8},{4,12},{8,0},{12,4},{16,24},{20,28},{24,16},{28,20},{1,9},{5... | collective-permute-start | bytes 1179656 | tf_op jit(solution)/shard_map/ppermute | solution.py:27
  44.3 48.9 %collective-permute-start.6 = (bf16[4,1,128,768]{3,2,0,1:T(8,128)(2,1)}, bf16[4,1,128,768]{3,2,0,1:T(8,128)(2,1)}, u32[]{:S(2)}, u32[]{:S(2)}) collective-permute-start(bf16[4,1,128,768]{3,2,0,1:T(8,128)(2,1)} %bitcast.15), channel_id=1, source_target_pairs={{0,16},{4,20},{8,24},{12,28},{16,0},{20,4},{24,8},{28,12},{1,17},{... | collective-permute-start | bytes 2359304 | tf_op jit(solution)/shard_map/ppermute | solution.py:27
  136.0 32.8 %collective-permute-start = (bf16[1,128,768]{1,2,0:T(8,128)(2,1)}, bf16[1,128,768]{1,2,0:T(8,128)(2,1)}, u32[]{:S(2)}, u32[]{:S(2)}) collective-permute-start(bf16[1,128,768]{1,2,0:T(8,128)(2,1)} %copy.66), channel_id=1, source_target_pairs={{28,0},{0,4},{4,8},{8,12},{12,16},{16,20},{20,24},{24,28},{29,1},{... | collective-permute-start | bytes 589832 | tf_op jit(solution)/shard_map/while/body/eval_jaxpr/ppermute | solution.py:37
  147.5 21.3 %collective-permute-start.1 = (bf16[1,128,768]{1,2,0:T(8,128)(2,1)}, bf16[1,128,768]{1,2,0:T(8,128)(2,1)}, u32[]{:S(2)}, u32[]{:S(2)}) collective-permute-start(bf16[1,128,768]{1,2,0:T(8,128)(2,1)} %copy.67), channel_id=1, source_target_pairs={{28,0},{0,4},{4,8},{8,12},{12,16},{16,20},{20,24},{24,28},{29,1},{... | collective-permute-start | bytes 589832 | tf_op jit(solution)/shard_map/while/body/eval_jaxpr/ppermute | solution.py:37
  170.4 21.0 %collective-permute-start = (bf16[1,128,768]{1,2,0:T(8,128)(2,1)}, bf16[1,128,768]{1,2,0:T(8,128)(2,1)}, u32[]{:S(2)}, u32[]{:S(2)}) collective-permute-start(bf16[1,128,768]{1,2,0:T(8,128)(2,1)} %copy.66), channel_id=1, source_target_pairs={{28,0},{0,4},{4,8},{8,12},{12,16},{16,20},{20,24},{24,28},{29,1},{... | collective-permute-start | bytes 589832 | tf_op jit(solution)/shard_map/while/body/eval_jaxpr/ppermute | solution.py:37
  172.0 19.3 %collective-permute-start.1 = (bf16[1,128,768]{1,2,0:T(8,128)(2,1)}, bf16[1,128,768]{1,2,0:T(8,128)(2,1)}, u32[]{:S(2)}, u32[]{:S(2)}) collective-permute-start(bf16[1,128,768]{1,2,0:T(8,128)(2,1)} %copy.67), channel_id=1, source_target_pairs={{28,0},{0,4},{4,8},{8,12},{12,16},{16,20},{20,24},{24,28},{29,1},{... | collective-permute-start | bytes 589832 | tf_op jit(solution)/shard_map/while/body/eval_jaxpr/ppermute | solution.py:37
  179.9 9.7 collective-permute-start.3
  193.0 21.0 %collective-permute-start = (bf16[1,128,768]{1,2,0:T(8,128)(2,1)}, bf16[1,128,768]{1,2,0:T(8,128)(2,1)}, u32[]{:S(2)}, u32[]{:S(2)}) collective-permute-start(bf16[1,128,768]{1,2,0:T(8,128)(2,1)} %copy.66), channel_id=1, source_target_pairs={{28,0},{0,4},{4,8},{8,12},{12,16},{16,20},{20,24},{24,28},{29,1},{... | collective-permute-start | bytes 589832 | tf_op jit(solution)/shard_map/while/body/eval_jaxpr/ppermute | solution.py:37
  194.6 19.3 %collective-permute-start.1 = (bf16[1,128,768]{1,2,0:T(8,128)(2,1)}, bf16[1,128,768]{1,2,0:T(8,128)(2,1)}, u32[]{:S(2)}, u32[]{:S(2)}) collective-permute-start(bf16[1,128,768]{1,2,0:T(8,128)(2,1)} %copy.67), channel_id=1, source_target_pairs={{28,0},{0,4},{4,8},{8,12},{12,16},{16,20},{20,24},{24,28},{29,1},{... | collective-permute-start | bytes 589832 | tf_op jit(solution)/shard_map/while/body/eval_jaxpr/ppermute | solution.py:37
  200.1 10.0 collective-permute-start.2
  201.1 11.1 collective-permute-start.3
  215.5 21.3 %collective-permute-start = (bf16[1,128,768]{1,2,0:T(8,128)(2,1)}, bf16[1,128,768]{1,2,0:T(8,128)(2,1)}, u32[]{:S(2)}, u32[]{:S(2)}) collective-permute-start(bf16[1,128,768]{1,2,0:T(8,128)(2,1)} %copy.66), channel_id=1, source_target_pairs={{28,0},{0,4},{4,8},{8,12},{12,16},{16,20},{20,24},{24,28},{29,1},{... | collective-permute-start | bytes 589832 | tf_op jit(solution)/shard_map/while/body/eval_jaxpr/ppermute | solution.py:37
  217.2 19.7 %collective-permute-start.1 = (bf16[1,128,768]{1,2,0:T(8,128)(2,1)}, bf16[1,128,768]{1,2,0:T(8,128)(2,1)}, u32[]{:S(2)}, u32[]{:S(2)}) collective-permute-start(bf16[1,128,768]{1,2,0:T(8,128)(2,1)} %copy.67), channel_id=1, source_target_pairs={{28,0},{0,4},{4,8},{8,12},{12,16},{16,20},{20,24},{24,28},{29,1},{... | collective-permute-start | bytes 589832 | tf_op jit(solution)/shard_map/while/body/eval_jaxpr/ppermute | solution.py:37
  223.9 9.2 collective-permute-start.2
  238.5 21.0 %collective-permute-start = (bf16[1,128,768]{1,2,0:T(8,128)(2,1)}, bf16[1,128,768]{1,2,0:T(8,128)(2,1)}, u32[]{:S(2)}, u32[]{:S(2)}) collective-permute-start(bf16[1,128,768]{1,2,0:T(8,128)(2,1)} %copy.66), channel_id=1, source_target_pairs={{28,0},{0,4},{4,8},{8,12},{12,16},{16,20},{20,24},{24,28},{29,1},{... | collective-permute-start | bytes 589832 | tf_op jit(solution)/shard_map/while/body/eval_jaxpr/ppermute | solution.py:37
  240.2 19.3 %collective-permute-start.1 = (bf16[1,128,768]{1,2,0:T(8,128)(2,1)}, bf16[1,128,768]{1,2,0:T(8,128)(2,1)}, u32[]{:S(2)}, u32[]{:S(2)}) collective-permute-start(bf16[1,128,768]{1,2,0:T(8,128)(2,1)} %copy.67), channel_id=1, source_target_pairs={{28,0},{0,4},{4,8},{8,12},{12,16},{16,20},{20,24},{24,28},{29,1},{... | collective-permute-start | bytes 589832 | tf_op jit(solution)/shard_map/while/body/eval_jaxpr/ppermute | solution.py:37
  261.1 21.0 %collective-permute-start = (bf16[1,128,768]{1,2,0:T(8,128)(2,1)}, bf16[1,128,768]{1,2,0:T(8,128)(2,1)}, u32[]{:S(2)}, u32[]{:S(2)}) collective-permute-start(bf16[1,128,768]{1,2,0:T(8,128)(2,1)} %copy.66), channel_id=1, source_target_pairs={{28,0},{0,4},{4,8},{8,12},{12,16},{16,20},{20,24},{24,28},{29,1},{... | collective-permute-start | bytes 589832 | tf_op jit(solution)/shard_map/while/body/eval_jaxpr/ppermute | solution.py:37
  262.7 19.3 %collective-permute-start.1 = (bf16[1,128,768]{1,2,0:T(8,128)(2,1)}, bf16[1,128,768]{1,2,0:T(8,128)(2,1)}, u32[]{:S(2)}, u32[]{:S(2)}) collective-permute-start(bf16[1,128,768]{1,2,0:T(8,128)(2,1)} %copy.67), channel_id=1, source_target_pairs={{28,0},{0,4},{4,8},{8,12},{12,16},{16,20},{20,24},{24,28},{29,1},{... | collective-permute-start | bytes 589832 | tf_op jit(solution)/shard_map/while/body/eval_jaxpr/ppermute | solution.py:37
  283.7 21.0 %collective-permute-start = (bf16[1,128,768]{1,2,0:T(8,128)(2,1)}, bf16[1,128,768]{1,2,0:T(8,128)(2,1)}, u32[]{:S(2)}, u32[]{:S(2)}) collective-permute-start(bf16[1,128,768]{1,2,0:T(8,128)(2,1)} %copy.66), channel_id=1, source_target_pairs={{28,0},{0,4},{4,8},{8,12},{12,16},{16,20},{20,24},{24,28},{29,1},{... | collective-permute-start | bytes 589832 | tf_op jit(solution)/shard_map/while/body/eval_jaxpr/ppermute | solution.py:37
  285.3 19.4 %collective-permute-start.1 = (bf16[1,128,768]{1,2,0:T(8,128)(2,1)}, bf16[1,128,768]{1,2,0:T(8,128)(2,1)}, u32[]{:S(2)}, u32[]{:S(2)}) collective-permute-start(bf16[1,128,768]{1,2,0:T(8,128)(2,1)} %copy.67), channel_id=1, source_target_pairs={{28,0},{0,4},{4,8},{8,12},{12,16},{16,20},{20,24},{24,28},{29,1},{... | collective-permute-start | bytes 589832 | tf_op jit(solution)/shard_map/while/body/eval_jaxpr/ppermute | solution.py:37
  306.3 21.0 %collective-permute-start = (bf16[1,128,768]{1,2,0:T(8,128)(2,1)}, bf16[1,128,768]{1,2,0:T(8,128)(2,1)}, u32[]{:S(2)}, u32[]{:S(2)}) collective-permute-start(bf16[1,128,768]{1,2,0:T(8,128)(2,1)} %copy.66), channel_id=1, source_target_pairs={{28,0},{0,4},{4,8},{8,12},{12,16},{16,20},{20,24},{24,28},{29,1},{... | collective-permute-start | bytes 589832 | tf_op jit(solution)/shard_map/while/body/eval_jaxpr/ppermute | solution.py:37
  307.9 19.3 %collective-permute-start.1 = (bf16[1,128,768]{1,2,0:T(8,128)(2,1)}, bf16[1,128,768]{1,2,0:T(8,128)(2,1)}, u32[]{:S(2)}, u32[]{:S(2)}) collective-permute-start(bf16[1,128,768]{1,2,0:T(8,128)(2,1)} %copy.67), channel_id=1, source_target_pairs={{28,0},{0,4},{4,8},{8,12},{12,16},{16,20},{20,24},{24,28},{29,1},{... | collective-permute-start | bytes 589832 | tf_op jit(solution)/shard_map/while/body/eval_jaxpr/ppermute | solution.py:37
  (111 other events, 537.2 us)
Sparse Core Ops, SparseCore 0:
  13.8 69.2 all-gather.4
  1032.2 30.4 all-gather.6
